TPU v7x, 512 devices: a whole 4x8x8 slice. The times are simulated.
512 devices in a mesh: row: 8 (over y), col: 64 (over z, x, core).
Axes of the slice: x: 4, y: 8, z: 8, core: 2. Of those that a mesh axis runs over, the one named last changes fastest.
Arguments:
- eigen_slab: float32 [8192, 65536], P('row', 'col'), may hold values from -6 to 6
- secular_poles: float32 [131072], P('col'), may hold values from 0 to 4, as said below
- coupling: float32 [131072], P('col'), may hold values from -7 to 7
- window_roots: float32 [128], replicated, may hold values from 0 to 4, as said below
- deflated: int32 [131072], P('col'), may hold values 0 or 1
- column_map: int32 [131072], P('col'), may hold values from 0 to 131071, as said below
Outputs:
- vectors: float32 [8192, 128], P(('row', 'col'))
Inputs may be any that keep to these rules, and one draw needn't show every extreme that they name: `column_map`: A permutation of the 131072 columns. Grid column c holds columns c * 1024 to (c + 1) * 1024 - 1 and 65536 + c * 1024 to 65536 + (c + 1) * 1024 - 1 of the slab, and positions c * 2048 to (c + 1) * 2048 - 1. Of one grid column's positions, exactly 64 map to the columns of one grid column, 32 to each of 62 others, none to the remaining one. `secular_poles`: each pole lies between (k + 0.2) * 4 / 256 and (k + 0.8) * 4 / 256 for a whole number k. `window_roots`: each root lies within 0.15 * 4 / 256 of k * 4 / 256 for a whole number k of 1 to 255.
All inputs are finite; a program needn't handle non-finite values. No bound on the sum of `deflated` on one device may be relied on, other than what follows from the above.
Results may differ from a plain program's by a relative error of at most 0.0003.
Values sent between devices are 32-bit elements; how exact they have to be, the bound alone decides.
A program may use at most 64 MiB of HBM per device.

v0:
```python
import jax
import jax.numpy as jnp
from jax import lax
from jax.sharding import PartitionSpec as P


def slot_plan(column_map, groups, cols_dev, capacity):
    block_len = column_map.shape[0]
    half_order = cols_dev * groups
    within = column_map % half_order
    target = within // cols_dev
    target_local = within % cols_dev + jnp.where(column_map >= half_order, cols_dev, 0)
    onehot = (target[:, None] == jnp.arange(groups, dtype=jnp.int32)[None, :]).astype(jnp.int32)
    slot_rank = jnp.sum(jnp.cumsum(onehot, axis=0) * onehot, axis=1) - 1
    slot_index = target * capacity + slot_rank
    sentinel = jnp.full((groups * capacity,), block_len, jnp.int32)
    slot_source = sentinel.at[slot_index].set(jnp.arange(block_len, dtype=jnp.int32))
    slot_target = sentinel.at[slot_index].set(target_local)
    return (slot_source, slot_target)


def route_rows(scaled, column_map, groups, cols_dev, capacity):
    slot_source, slot_target = slot_plan(column_map, groups, cols_dev, capacity)
    outgoing = jnp.take(scaled, slot_source, axis=0, mode="fill", fill_value=0.0)
    outgoing = outgoing.reshape(groups, capacity, scaled.shape[1])
    arrived, arrived_index = (
        lax.all_to_all(outgoing, "col", split_axis=0, concat_axis=0, tiled=True),
        lax.all_to_all(
            slot_target.reshape(groups, capacity), "col", split_axis=0, concat_axis=0, tiled=True
        ),
    )
    flat_rows = arrived.reshape(groups * capacity, scaled.shape[1])
    return jnp.zeros_like(scaled).at[arrived_index.reshape(-1)].set(flat_rows, mode="drop")


def body(eigen_slab, secular_poles, coupling, window_roots, deflated, column_map):
    groups = lax.axis_size("col")
    row_groups = lax.axis_size("row")
    block_len = secular_poles.shape[0]
    cols_dev = eigen_slab.shape[1]
    capacity = 2 * (block_len // groups)
    distance = secular_poles[:, None] - window_roots[None, :]
    entries = jnp.where(
        deflated[:, None] == 0, coupling[:, None] / distance, jnp.zeros_like(distance)
    )
    sum_squares = lax.psum(jnp.sum(entries * entries, axis=0), "col")
    inverse = lax.rsqrt(sum_squares)
    scaled = entries * inverse[None, :]
    placed = route_rows(scaled, column_map, groups, cols_dev, capacity)
    half_start = jnp.where(lax.axis_index("row") < row_groups // 2, 0, cols_dev)
    half_window = lax.dynamic_slice_in_dim(placed, half_start, cols_dev, 0)
    return lax.psum_scatter(
        jnp.dot(
            eigen_slab,
            half_window,
            precision=lax.Precision.HIGHEST,
            preferred_element_type=jnp.float32,
        ),
        "col",
        scatter_dimension=0,
        tiled=True,
    )


def solution(mesh):
    return jax.shard_map(
        body,
        mesh=mesh,
        in_specs=(P("row", "col"), P("col"), P("col"), P(), P("col"), P("col")),
        out_specs=P(("row", "col"), None),
        check_vma=False,
    )
```

profile of v0, /device:TPU:8, one launch (start us, length us, event | category | flops | bytes accessed | tf_op | source)
XLA Modules:
  0.0 474.1 jit_solution(13782609337282554614)
XLA Ops:
  6.5 0.7 fusion.9
  7.3 18.1 %reduce-window.6 = s32[64,16,128]{2,1,0:T(8,128)S(1)} reduce-window(s32[64,16,128]{2,1,0:T(8,128)S(1)} %fusion.6, s32[]{:T(128)} %constant.68.clone.1), window={size=1x1x128 pad=0_0x0_0x127_0}, to_apply=%region_0.1 | reduce-window | flops 16646144 | bytes 1048580 | tf_op jit(solution)/shard_map/reduce-window
  25.5 0.2 slice.10
  25.7 0.4 copy.14
  26.3 0.2 broadcast_add_fusion
  26.7 8.1 %scatter_custom_fusion = s32[4096]{0:T(1024)S(1)} fusion(s32[2048]{0:T(1024)S(1)} %compare_select_fusion.2, s32[2048]{0:T(1024)S(1)} %get-tuple-element.5, s32[]{:T(128)} %constant.67.clone.1), kind=kCustom, calls=%fused_computation.37 | custom fusion | bytes 16388 | tf_op jit(solution)/shard_map/scatter | solution.py:18
  34.8 0.7 all_to_all.9
  35.5 13.8 %all-to-all-start = ((s32[64,1,64]{2,1,0:T(1,128)}), s32[64,1,64]{2,1,0:T(1,128)S(1)}, u32[]{:S(2)}, u32[]{:S(2)}) async-start(s32[64,1,64]{2,1,0:T(1,128)} %all_to_all.9), calls=%async_computation | async-start | bytes 65536 | tf_op jit(solution)/shard_map/all_to_all | solution.py:28
  49.3 8.1 %scatter_custom_fusion.1 = s32[4096]{0:T(1024)S(1)} fusion(s32[2048]{0:T(1024)S(1)} %compare_select_fusion.2, s32[2048]{0:T(1024)S(1)} %iota.11, s32[]{:T(128)} %constant.67.clone.1), kind=kCustom, calls=%fused_computation.35 | custom fusion | bytes 16388 | tf_op jit(solution)/shard_map/scatter | solution.py:17
  57.5 1.0 multiply_reduce_fusion
  58.4 129.0 %psum.7 = f32[128]{0:T(128)S(1)} all-reduce(f32[128]{0:T(128)S(1)} %multiply_reduce_fusion), channel_id=1, replica_groups=mesh['row'=8,'col'=64] {'col'}, use_global_device_ids=true, to_apply=%region_6.7 | all-reduce | flops 128 | bytes 1024 | tf_op jit(solution)/shard_map/psum | solution.py:46
  187.4 0.9 fusion
  188.4 10.8 %gather_fusion = f32[4096,128]{1,0:T(8,128)S(1)} fusion(f32[2048,128]{1,0:T(8,128)S(1)} %fusion, s32[4096]{0:T(1024)S(1)} %fusion.7), kind=kCustom, calls=%fused_computation | custom fusion | bytes 4210688 | tf_op jit(solution)/shard_map/jit(_take)/gather | solution.py:24
  199.2 1.7 broadcast_select_fusion
  200.9 5.3 %all-to-all-start.1 = ((f32[64,64,128]{2,1,0:T(8,128)}), f32[64,64,128]{2,1,0:T(8,128)S(1)}, u32[]{:S(2)}, u32[]{:S(2)}) async-start(f32[64,64,128]{2,1,0:T(8,128)} %broadcast_select_fusion), calls=%async_computation.1 | async-start | bytes 4194304 | tf_op jit(solution)/shard_map/all_to_all | solution.py:27
  206.3 0.5 broadcast.104
  206.8 0.7 reduce.3
  207.7 49.9 %all-to-all-done.1 = f32[64,64,128]{2,1,0:T(8,128)S(1)} async-done(((f32[64,64,128]{2,1,0:T(8,128)}), f32[64,64,128]{2,1,0:T(8,128)S(1)}, u32[]{:S(2)}, u32[]{:S(2)}) %all-to-all-start.1) | async-done | bytes 2097184 | tf_op jit(solution)/shard_map/all_to_all | solution.py:27
  257.6 11.0 %scatter_custom_fusion.2 = f32[2048,128]{1,0:T(8,128)S(1)} fusion(s32[4096]{0:T(1024)S(1)} %bitcast.32, f32[4096,128]{1,0:T(8,128)S(1)} %bitcast.27, f32[]{:T(128)} %constant.66.clone.1), kind=kCustom, calls=%fused_computation.15 | custom fusion | bytes 1048580 | tf_op jit(solution)/shard_map/scatter | solution.py:33
  268.7 7.5 %convolution_bitcast_fusion = f32[1024,128]{0,1:T(8,128)} fusion(f32[1024,1024]{1,0:T(8,128)} %param.6, f32[2048,128]{1,0:T(8,128)S(1)} %scatter_custom_fusion.2, s32[]{:T(128)S(6)} %select_n.62), kind=kOutput, calls=%fused_computation.4 | convolution fusion | flops 1610612736 | bytes 5242884 | tf_op jit(solution)/shard_map/dot_general | solution.py:53
  276.2 1.3 dynamic-slice
  278.1 187.6 %all-reduce.3.cloned.1.call-done = f32[1024,128]{0,1:T(8,128)} async-done(((f32[1024,128]{0,1:T(8,128)}), f32[1024,128]{0,1:T(8,128)}) %all-reduce.3.cloned.1.call-update) | async-done | bytes 524304
  465.7 0.9 constant_dynamic-slice_fusion
  466.6 0.7 copy.13
  (23 shorter events, 0.7 us)
Async XLA Ops:
  7.3 50.1 %copy-start.2 = (s32[2048]{0:T(1024)S(1)}, s32[2048]{0:T(1024)}, u32[]{:S(2)}) copy-start(s32[2048]{0:T(1024)} %param.10) | copy-start | bytes 24580
  7.3 50.1 %copy-start = (f32[2048]{0:T(1024)S(1)}, f32[2048]{0:T(1024)}, u32[]{:S(2)}) copy-start(f32[2048]{0:T(1024)} %param.7) | copy-start | bytes 24580
  7.3 50.1 %copy-start.1 = (f32[2048]{0:T(1024)S(1)}, f32[2048]{0:T(1024)}, u32[]{:S(2)}) copy-start(f32[2048]{0:T(1024)} %param.8) | copy-start | bytes 24580
  7.3 50.1 %copy-start.3 = (f32[128]{0:T(128)S(1)}, f32[128]{0:T(128)}, u32[]{:S(2)}) copy-start(f32[128]{0:T(128)} %param.9) | copy-start | bytes 1540
  35.5 165.4 %all-to-all-start = ((s32[64,1,64]{2,1,0:T(1,128)}), s32[64,1,64]{2,1,0:T(1,128)S(1)}, u32[]{:S(2)}, u32[]{:S(2)}) async-start(s32[64,1,64]{2,1,0:T(1,128)} %all_to_all.9), calls=%async_computation | async-start | bytes 65536 | tf_op jit(solution)/shard_map/all_to_all | solution.py:28
  200.9 56.7 %all-to-all-start.1 = ((f32[64,64,128]{2,1,0:T(8,128)}), f32[64,64,128]{2,1,0:T(8,128)S(1)}, u32[]{:S(2)}, u32[]{:S(2)}) async-start(f32[64,64,128]{2,1,0:T(8,128)} %broadcast_select_fusion), calls=%async_computation.1 | async-start | bytes 4194304 | tf_op jit(solution)/shard_map/all_to_all | solution.py:27
  206.3 259.4 %all-reduce.3.cloned.1.call-start = ((), (), s32[]{:S(2)}) async-start(), calls=%async_computation.2 | async-start | bytes 1048576
Sparse Core Ops, SparseCore 0:
  276.3 189.3 all-reduce.2
where the time goes:
time: 475 us; the launch traced here: 474 us
  waiting for transfers between devices  238 us (50%)
  blocking collectives  129 us (27%)
  local copies, waits for them, and re-layouts  42.8 us (9%)
  other arithmetic  23.9 us (5%)
  starting transfers between devices  19.2 us (4%)
  between operations  14.3 us (3%)
  matrix products  7.48 us (2%)
    unnamed x2, waiting for transfers between devices  188 us
    psum x1, blocking collectives, body(): sum_squares = lax.psum(jnp.sum(entries * entries, axis=0), 'col')  129 us
    all_to_all x1, waiting for transfers between devices, route_rows(): lax.all_to_all(outgoing, 'col', split_axis=0, concat_axis=0, tiled=True)  49.9 us
    another operation x3, other arithmetic  18.5 us
    all_to_all x1, starting transfers between devices, route_rows(): lax.all_to_all(slot_target.reshape(groups, capacity), 'col', split_axis=0...  13.8 us
    scatter x1, local copies, waits for them, and re-layouts, route_rows(): jnp.zeros_like(scaled).at[arrived_index.reshape(-1)]  11 us
    gather x1, local copies, waits for them, and re-layouts, route_rows(): jnp.take(scaled, slot_source, axis=0, mode='fill', fill_value=0.0)  10.8 us
  transfers between devices with their start and end apart: 3, of which 2 were waited for; matrix products, arithmetic and copies ran while one was open for 5% of the time, Pallas kernels for 0%

commit v1 on v0

--- a/solution.py
+++ b/solution.py
@@ -43,7 +43,9 @@
     entries = jnp.where(
         deflated[:, None] == 0, coupling[:, None] / distance, jnp.zeros_like(distance)
     )
-    sum_squares = lax.psum(jnp.sum(entries * entries, axis=0), "col")
+    own = jnp.sum(entries * entries, axis=0)
+    parts = lax.all_gather(own, "col", axis=0, tiled=False)
+    sum_squares = parts.sum(axis=0)
     inverse = lax.rsqrt(sum_squares)
     scaled = entries * inverse[None, :]
     placed = route_rows(scaled, column_map, groups, cols_dev, capacity)

time: 475 us -> 388 us (0.82)
  blocking collectives: 129 us -> 41 us
    psum x1 -> x0, blocking collectives: 129 us -> none  [body(): sum_squares = lax.psum(jnp.sum(entries * entries, axis=0), 'col')]
    all_gather x0 -> x1, blocking collectives: none -> 41 us  [body(): parts = lax.all_gather(own, 'col', axis=0, tiled=False)]
  transfers between devices with their start and end apart: 3 -> 3, of which waited for: 2 -> 2; matrix products, arithmetic and copies ran while one was open for 5% -> 7% of each run, Pallas kernels for 0% -> 0%
where the time goes in v1:
time: 388 us
  waiting for transfers between devices  238 us (61%)
  local copies, waits for them, and re-layouts  42.8 us (11%)
  blocking collectives  41 us (11%)
  other arithmetic  23.9 us (6%)
  starting transfers between devices  20.6 us (5%)
  between operations  14.3 us (4%)
  matrix products  7.48 us (2%)
    unnamed x2, waiting for transfers between devices  188 us
    all_to_all x1, waiting for transfers between devices, route_rows(): lax.all_to_all(outgoing, 'col', split_axis=0, concat_axis=0, tiled=True)  49.9 us
    all_gather x1, blocking collectives, body(): parts = lax.all_gather(own, 'col', axis=0, tiled=False)  41 us
    another operation x3, other arithmetic  18.5 us
    all_to_all x1, starting transfers between devices, route_rows(): lax.all_to_all(slot_target.reshape(groups, capacity), 'col', split_axis=0...  13.8 us
    scatter x1, local copies, waits for them, and re-layouts, route_rows(): jnp.zeros_like(scaled).at[arrived_index.reshape(-1)]  11 us
    gather x1, local copies, waits for them, and re-layouts, route_rows(): jnp.take(scaled, slot_source, axis=0, mode='fill', fill_value=0.0)  10.8 us
    scatter x1, local copies, waits for them, and re-layouts, slot_plan(): slot_target = sentinel.at[slot_index].set(target_local)  8.06 us
  transfers between devices with their start and end apart: 3, of which 2 were waited for; matrix products, arithmetic and copies ran while one was open for 7% of the time, Pallas kernels for 0%

profile of v1, /device:TPU:8, one launch (start us, length us, event | category | flops | bytes accessed | tf_op | source)
XLA Modules:
  0.0 387.9 jit_solution(18025468665197989754)
XLA Ops:
  6.5 0.7 fusion.9
  7.3 18.1 %reduce-window.6 = s32[64,16,128]{2,1,0:T(8,128)S(1)} reduce-window(s32[64,16,128]{2,1,0:T(8,128)S(1)} %fusion.6, s32[]{:T(128)} %constant.68.clone.1), window={size=1x1x128 pad=0_0x0_0x127_0}, to_apply=%region_0.1 | reduce-window | flops 16646144 | bytes 1048580 | tf_op jit(solution)/shard_map/reduce-window
  25.5 0.2 slice.10
  25.7 0.4 copy.14
  26.3 0.2 broadcast_add_fusion
  26.7 8.1 %scatter_custom_fusion = s32[4096]{0:T(1024)S(1)} fusion(s32[2048]{0:T(1024)S(1)} %compare_select_fusion.2, s32[2048]{0:T(1024)S(1)} %get-tuple-element.5, s32[]{:T(128)} %constant.67.clone.1), kind=kCustom, calls=%fused_computation.37 | custom fusion | bytes 16388 | tf_op jit(solution)/shard_map/scatter | solution.py:18
  34.8 0.7 all_to_all.9
  35.5 13.8 %all-to-all-start = ((s32[64,1,64]{2,1,0:T(1,128)}), s32[64,1,64]{2,1,0:T(1,128)S(1)}, u32[]{:S(2)}, u32[]{:S(2)}) async-start(s32[64,1,64]{2,1,0:T(1,128)} %all_to_all.9), calls=%async_computation | async-start | bytes 65536 | tf_op jit(solution)/shard_map/all_to_all | solution.py:28
  49.3 8.1 %scatter_custom_fusion.1 = s32[4096]{0:T(1024)S(1)} fusion(s32[2048]{0:T(1024)S(1)} %compare_select_fusion.2, s32[2048]{0:T(1024)S(1)} %iota.11, s32[]{:T(128)} %constant.67.clone.1), kind=kCustom, calls=%fused_computation.35 | custom fusion | bytes 16388 | tf_op jit(solution)/shard_map/scatter | solution.py:17
  57.5 1.0 multiply_reduce_fusion
  58.4 41.0 %all-gather.1 = f32[64,1,128]{2,1,0:T(1,128)S(1)} all-gather(f32[1,1,128]{2,1,0:T(1,128)S(1)} %bitcast.34), channel_id=2, replica_groups=mesh['row'=8,'col'=64] {'col'}, dimensions={0}, use_global_device_ids=true | all-gather | bytes 33280 | tf_op jit(solution)/shard_map/all_gather | solution.py:47
  99.5 0.9 fusion
  100.5 10.8 %gather_fusion = f32[4096,128]{1,0:T(8,128)S(1)} fusion(f32[2048,128]{1,0:T(8,128)S(1)} %fusion, s32[4096]{0:T(1024)S(1)} %fusion.7), kind=kCustom, calls=%fused_computation | custom fusion | bytes 4210688 | tf_op jit(solution)/shard_map/jit(_take)/gather | solution.py:24
  111.3 1.7 broadcast_select_fusion
  113.0 6.7 %all-to-all-start.1 = ((f32[64,64,128]{2,1,0:T(8,128)}), f32[64,64,128]{2,1,0:T(8,128)S(1)}, u32[]{:S(2)}, u32[]{:S(2)}) async-start(f32[64,64,128]{2,1,0:T(8,128)} %broadcast_select_fusion), calls=%async_computation.1 | async-start | bytes 4194304 | tf_op jit(solution)/shard_map/all_to_all | solution.py:27
  119.8 0.5 broadcast.103
  120.3 0.7 reduce.4
  121.2 49.9 %all-to-all-done.1 = f32[64,64,128]{2,1,0:T(8,128)S(1)} async-done(((f32[64,64,128]{2,1,0:T(8,128)}), f32[64,64,128]{2,1,0:T(8,128)S(1)}, u32[]{:S(2)}, u32[]{:S(2)}) %all-to-all-start.1) | async-done | bytes 2097184 | tf_op jit(solution)/shard_map/all_to_all | solution.py:27
  171.1 11.0 %scatter_custom_fusion.2 = f32[2048,128]{1,0:T(8,128)S(1)} fusion(s32[4096]{0:T(1024)S(1)} %bitcast.33, f32[4096,128]{1,0:T(8,128)S(1)} %bitcast.28, f32[]{:T(128)} %constant.66.clone.1), kind=kCustom, calls=%fused_computation.15 | custom fusion | bytes 1048580 | tf_op jit(solution)/shard_map/scatter | solution.py:33
  182.2 7.5 %convolution_bitcast_fusion = f32[1024,128]{0,1:T(8,128)} fusion(f32[1024,1024]{1,0:T(8,128)} %param.6, f32[2048,128]{1,0:T(8,128)S(1)} %scatter_custom_fusion.2, s32[]{:T(128)S(6)} %select_n.62), kind=kOutput, calls=%fused_computation.4 | convolution fusion | flops 1610612736 | bytes 5242884 | tf_op jit(solution)/shard_map/dot_general | solution.py:55
  189.7 1.3 dynamic-slice
  191.6 187.9 %all-reduce.3.cloned.1.call-done = f32[1024,128]{0,1:T(8,128)} async-done(((f32[1024,128]{0,1:T(8,128)}), f32[1024,128]{0,1:T(8,128)}) %all-reduce.3.cloned.1.call-update) | async-done | bytes 524304
  379.5 0.9 constant_dynamic-slice_fusion
  380.4 0.7 copy.13
  (24 shorter events, 0.8 us)
Async XLA Ops:
  7.3 50.1 %copy-start.2 = (s32[2048]{0:T(1024)S(1)}, s32[2048]{0:T(1024)}, u32[]{:S(2)}) copy-start(s32[2048]{0:T(1024)} %param.10) | copy-start | bytes 24580
  7.3 50.1 %copy-start = (f32[2048]{0:T(1024)S(1)}, f32[2048]{0:T(1024)}, u32[]{:S(2)}) copy-start(f32[2048]{0:T(1024)} %param.7) | copy-start | bytes 24580
  7.3 50.1 %copy-start.1 = (f32[2048]{0:T(1024)S(1)}, f32[2048]{0:T(1024)}, u32[]{:S(2)}) copy-start(f32[2048]{0:T(1024)} %param.8) | copy-start | bytes 24580
  7.3 50.1 %copy-start.3 = (f32[128]{0:T(128)S(1)}, f32[128]{0:T(128)}, u32[]{:S(2)}) copy-start(f32[128]{0:T(128)} %param.9) | copy-start | bytes 1540
  35.5 77.5 %all-to-all-start = ((s32[64,1,64]{2,1,0:T(1,128)}), s32[64,1,64]{2,1,0:T(1,128)S(1)}, u32[]{:S(2)}, u32[]{:S(2)}) async-start(s32[64,1,64]{2,1,0:T(1,128)} %all_to_all.9), calls=%async_computation | async-start | bytes 65536 | tf_op jit(solution)/shard_map/all_to_all | solution.py:28
  113.0 58.1 %all-to-all-start.1 = ((f32[64,64,128]{2,1,0:T(8,128)}), f32[64,64,128]{2,1,0:T(8,128)S(1)}, u32[]{:S(2)}, u32[]{:S(2)}) async-start(f32[64,64,128]{2,1,0:T(8,128)} %broadcast_select_fusion), calls=%async_computation.1 | async-start | bytes 4194304 | tf_op jit(solution)/shard_map/all_to_all | solution.py:27
  119.8 259.7 %all-reduce.3.cloned.1.call-start = ((), (), s32[]{:S(2)}) async-start(), calls=%async_computation.2 | async-start | bytes 1048576
Sparse Core Ops, SparseCore 0:
  189.8 189.6 all-reduce.2
